TPU v7x, 256 devices: a whole 4x4x8 slice. The times are simulated.
256 devices in a mesh: site: 4 (over x), fsdp: 64 (over z, y, core).
Axes of the slice: x: 4, y: 4, z: 8, core: 2. Of those that a mesh axis runs over, the one named last changes fastest.
Arguments:
- held_input: bfloat16 [4, 32768, 1536], P('site', 'fsdp'), may hold values from -16 to 16
- held_cotangent: bfloat16 [4, 32768, 1536], P('site', 'fsdp'), may hold values from -6 to 6
- proj_weight: bfloat16 [1536, 1536], P('fsdp'), may hold values from -0.15625 to 0.15625
- stem_weight: bfloat16 [3, 512, 1536], P(None, 'fsdp'), may hold values from -0.15625 to 0.15625
- seg_counts: int32 [4, 64], P('site'), may hold values from 1 to 128, 4096 in all within a row
Outputs:
- stem_grad: bfloat16 [4, 131072, 512], P('site', 'fsdp')
- weight_grad: float32 [1536, 1536], P('fsdp')
Inputs may be any that keep to these rules, and one draw needn't show every extreme that they name: `seg_counts`: in every group the 64 counts sum to 4096, so that every holder slot is used; one owner has exactly 128, and a holder keeps at most 2 segments of one owner, a bound reached in every draw.
All inputs are finite; a program needn't handle non-finite values.
Results may differ from a plain program's by a relative error of at most 0.0049.
Values may be sent and summed in bfloat16 or wider, within the bound.
A program may use at most 128 MiB of HBM per device.

v0:
```python
import math
import jax
import jax.numpy as jnp
from jax import lax
from jax.sharding import PartitionSpec as P

D = 1536
SEG = 8
HOLD = 64
OWN_SEG = 128
EPSILON = 1e-05


def stem_taps(frames, stem_weight):
    return jnp.einsum(
        "rd,kcd->krc",
        frames,
        lax.all_gather(stem_weight, "fsdp", axis=1, tiled=True),
        preferred_element_type=jnp.float32,
    )


def body(held_input, held_cotangent, proj_weight, stem_weight, seg_counts):
    group_size = lax.axis_size("fsdp")
    capacity = 2 * ((OWN_SEG + 2 * group_size - 1) // (2 * group_size))
    my_index = lax.axis_index("fsdp")
    inputs = held_input[0].astype(jnp.float32)
    cotangent = held_cotangent[0]
    row_mean = jnp.mean(inputs, axis=-1, keepdims=True)
    centered = inputs - row_mean
    variance = jnp.mean(centered * centered, axis=-1, keepdims=True)
    inverse = lax.rsqrt(variance + EPSILON)
    normed = centered * inverse
    normed_bf = normed.astype(jnp.bfloat16)
    proj_back = lax.dot_general(
        cotangent,
        lax.all_gather(proj_weight, "fsdp", axis=0, tiled=True),
        (((1,), (1,)), ((), ())),
        preferred_element_type=jnp.float32,
    )
    input_grad = cotangent.astype(jnp.float32) + inverse * (
        proj_back
        - jnp.mean(proj_back, axis=-1, keepdims=True)
        - normed * jnp.mean(proj_back * normed, axis=-1, keepdims=True)
    )
    input_grad = input_grad.astype(jnp.bfloat16)
    counts = seg_counts[0]
    endings = jnp.cumsum(counts)
    starts = endings - counts
    slot_ids = jnp.arange(HOLD, dtype=jnp.int32)
    item_index = 2 * (slot_ids // 2 * group_size + my_index) + slot_ids % 2
    owner_ids = jnp.sum((item_index[:, None] >= endings[None, :]).astype(jnp.int32), axis=1)
    earlier = (slot_ids[None, :] < slot_ids[:, None]) & (owner_ids[None, :] == owner_ids[:, None])
    rank_ids = jnp.sum(earlier.astype(jnp.int32), axis=1)
    target = owner_ids * capacity + rank_ids
    positions = jnp.arange(group_size * capacity, dtype=jnp.int32)
    matched = target[None, :] == positions[:, None]
    filled = jnp.any(matched, axis=1)
    source = jnp.sum(jnp.where(matched, slot_ids[None, :], 0), axis=1)
    owner_hit = jnp.arange(group_size, dtype=jnp.int32) == my_index
    my_count = jnp.sum(jnp.where(owner_hit, counts, 0))
    my_start = jnp.sum(jnp.where(owner_hit, starts, 0))
    segment = jnp.arange(OWN_SEG, dtype=jnp.int32)
    is_live = segment < my_count
    holder = (my_start + segment) // 2 % group_size
    before = (
        (segment[None, :] < segment[:, None])
        & (holder[None, :] == holder[:, None])
        & is_live[None, :]
    )
    holder_rank = jnp.sum(before.astype(jnp.int32), axis=1)
    row_index = jnp.where(is_live, holder * capacity + holder_rank, 0)
    held_segments = input_grad.reshape(HOLD, SEG, D)
    zero_bf = jnp.zeros((), jnp.bfloat16)
    send_rows = jnp.where(filled[:, None, None], jnp.take(held_segments, source, axis=0), zero_bf)
    received = lax.all_to_all(
        send_rows.reshape(group_size, capacity, SEG, D),
        "fsdp",
        split_axis=0,
        concat_axis=0,
        tiled=True,
    )
    picked = jnp.take(received.reshape(group_size * capacity, SEG, D), row_index, axis=0)
    frames = jnp.where(is_live[:, None, None], picked, zero_bf).reshape(OWN_SEG * SEG, D)
    tap_terms = stem_taps(frames, stem_weight)
    shifted = jnp.concatenate(
        [tap_terms[0][1:], jnp.zeros((1, tap_terms.shape[2]), jnp.float32)], 0
    )
    odd_rows = tap_terms[2] + shifted
    stem_rows = (
        jnp.stack([tap_terms[1], odd_rows], 1)
        .reshape(2 * OWN_SEG * SEG, tap_terms.shape[2])
        .astype(jnp.bfloat16)
    )
    shard_sum = lax.psum_scatter(
        lax.dot_general(
            normed_bf, cotangent, (((0,), (0,)), ((), ())), preferred_element_type=jnp.float32
        ),
        "fsdp",
        scatter_dimension=0,
        tiled=True,
    )
    shard_sum = lax.psum(shard_sum, "site")
    weight_grad = shard_sum / math.sqrt(lax.axis_size("site") * group_size * HOLD * SEG)
    return (stem_rows[None], weight_grad)


def solution(mesh):
    placed = (
        P("site", "fsdp", None),
        P("site", "fsdp", None),
        P("fsdp", None),
        P(None, "fsdp", None),
        P("site", None),
    )
    return jax.shard_map(
        body,
        mesh=mesh,
        in_specs=placed,
        out_specs=(P("site", "fsdp", None), P("fsdp", None)),
        check_vma=False,
    )
```

profile of v0, /device:TPU:1, one launch (start us, length us, event | category | flops | bytes accessed | tf_op | source)
XLA Modules:
  0.0 408.3 jit_solution(15506953780961973677)
XLA Ops:
  7.2 1.8 convert_reduce_fusion
  9.1 2.0 fusion.10
  11.1 5.3 %fusion.25 = f32[1536,1536]{1,0:T(8,128)} fusion(bf16[1,512,1536]{2,1,0:T(8,128)(2,1)S(1)} %copy-done, bf16[1,512,1536]{2,1,0:T(8,128)(2,1)S(1)} %copy-done.1, f32[512]{0:T(512)S(1)} %add_rsqrt_fusion, f32[512]{0:T(512)S(1)} %broadcast_multiply_fusion.3), kind=kOutput, calls=%fused_computation.33 | convolution fusion | flops 2419064832 | bytes 12587008 | tf_op jit(solution)/shard_map/dot_general | solution.py:96
  16.5 0.7 all-gather.3.cloned.1.call-update
  17.2 152.7 %reduce-scatter.4.cloned.1.call-done = f32[24,1536]{1,0:T(8,128)} async-done(((f32[1536,1536]{1,0:T(8,128)}), f32[24,1536]{1,0:T(8,128)}) %reduce-scatter.4.cloned.1.call-update) | async-done | bytes 147472
  170.8 0.6 fusion.45
  172.4 83.0 %all-gather.3.cloned.1.call-done = bf16[1536,1536]{1,0:T(8,128)(2,1)} async-done(((bf16[24,1536]{1,0:T(8,128)(2,1)}), bf16[1536,1536]{1,0:T(8,128)(2,1)}) %all-gather.3.cloned.1.call-update) | async-done | bytes 4718608 | tf_op jit(solution)/shard_map/all_gather | solution.py:37
  255.4 4.9 %fusion.55 = (f32[512]{0:T(512)S(1)}, f32[512]{0:T(512)S(1)}, f32[512,1536]{1,0:T(8,128)S(1)}) fusion(f32[512]{0:T(512)S(1)} %add_rsqrt_fusion, f32[512]{0:T(512)S(1)} %broadcast_multiply_fusion.3, bf16[1,512,1536]{2,1,0:T(8,128)(2,1)S(1)} %copy-done, bf16[1536,1536]{1,0:T(8,128)(2,1)} %all-gather.3.cloned.1.call-done, bf16[1,512,1536]{2,1,0:T(8,128)(2,1)S(1)} %copy-done.1), kind=kOutput, calls=%fused_computation.107 | convolution fusion | flops 2420636672 | bytes 11018240 | tf_op jit(solution)/shard_map/dot_general | solution.py:35
  260.3 1.2 fusion.27
  261.5 2.5 gather_fusion
  264.0 3.3 select_select_fusion
  267.3 6.3 %all-to-all-start = ((bf16[64,2,8,1536]{3,2,1,0:T(8,128)(2,1)}), bf16[64,2,8,1536]{3,2,1,0:T(8,128)(2,1)S(1)}, u32[]{:S(2)}, u32[]{:S(2)}) async-start(bf16[64,2,8,1536]{3,2,1,0:T(8,128)(2,1)} %select_select_fusion), calls=%async_computation | async-start | bytes 6291456 | tf_op jit(solution)/shard_map/all_to_all | solution.py:76
  273.6 0.7 iota_compare_fusion.3
  274.3 0.7 and_select_fusion.4
  275.1 1.3 compare_and_fusion.1
  276.8 1.3 fusion.52
  278.2 21.2 %all-reduce.4.cloned.1.call-done = f32[24,1536]{1,0:T(8,128)} async-done(((f32[24,1536]{1,0:T(8,128)}), f32[24,1536]{1,0:T(8,128)}) %all-reduce.4.cloned.1.call-update) | async-done | bytes 147472 | tf_op jit(solution)/shard_map/psum | solution.py:103
  299.4 1.6 broadcast_multiply_fusion
  300.9 48.2 %all-to-all-done = bf16[64,2,8,1536]{3,2,1,0:T(8,128)(2,1)S(1)} async-done(((bf16[64,2,8,1536]{3,2,1,0:T(8,128)(2,1)}), bf16[64,2,8,1536]{3,2,1,0:T(8,128)(2,1)S(1)}, u32[]{:S(2)}, u32[]{:S(2)}) %all-to-all-start) | async-done | bytes 3145760 | tf_op jit(solution)/shard_map/all_to_all | solution.py:76
  349.1 2.4 gather_fusion.1
  351.5 36.3 %all-gather.5.cloned.1.call-done = bf16[3,512,1536]{2,1,0:T(8,128)(2,1)} async-done(((bf16[3,8,1536]{2,1,0:T(8,128)(2,1)}), bf16[3,512,1536]{2,1,0:T(8,128)(2,1)}) %all-gather.5.cloned.1.call-update) | async-done | bytes 4718608 | tf_op jit(solution)/shard_map/all_gather | solution.py:18
  387.9 8.4 %fusion.19 = f32[3,1024,512]{2,1,0:T(8,128)S(1)} fusion(bf16[3,512,1536]{2,1,0:T(8,128)(2,1)} %all-gather.5.cloned.1.call-done, bf16[128,8,1536]{2,1,0:T(8,128)(2,1)} %gather_fusion.1, pred[1024]{0:T(1024)(128)(4,1)S(1)} %broadcast_in_dim.96, pred[1024]{0:T(1024)(128)(4,1)S(1)} %broadcast_in_dim.93), kind=kOutput, calls=%fused_computation.25 | convolution fusion | flops 4834983936 | bytes 14157824 | tf_op jit(solution)/shard_map/rd,kcd->krc/dot_general | solution.py:15
  397.4 2.2 copy.13
  399.6 2.2 convert_element_type.46
  (41 shorter events, 3.6 us)
Async XLA Ops:
  7.2 3.9 copy-start
  7.2 3.9 copy-start.1
  7.2 162.7 %reduce-scatter.4.cloned.1.call-start = ((), (), s32[]{:S(2)}) async-start(), calls=%async_computation.5 | async-start | bytes 9584640
  16.4 154.1 %copy-start.3 = (s32[1,64]{1,0:T(1,128)S(1)}, s32[1,64]{1,0:T(1,128)}, u32[]{:S(2)}) copy-start(s32[1,64]{1,0:T(1,128)} %param.9) | copy-start | bytes 772
  16.4 239.0 %all-gather.3.cloned.1.call-start = ((), (), s32[]{:S(2)}) async-start(), calls=%async_computation.2 | async-start | bytes 4792320 | tf_op jit(solution)/shard_map/all_gather | solution.py:37
  17.2 282.2 %all-reduce.4.cloned.1.call-start = ((), (), s32[]{:S(2)}) async-start(), calls=%async_computation.4 | async-start | bytes 294912 | tf_op jit(solution)/shard_map/psum | solution.py:103
  169.9 217.9 %all-gather.5.cloned.1.call-start = ((), (), s32[]{:S(2)}) async-start(), calls=%async_computation.3 | async-start | bytes 4792320 | tf_op jit(solution)/shard_map/all_gather | solution.py:18
  255.4 4.9 %copy-start.2 = (bf16[1,512,1536]{2,1,0:T(8,128)(2,1)S(1)}, bf16[1,512,1536]{2,1,0:T(8,128)(2,1)}, u32[]{:S(2)}) copy-start(bf16[1,512,1536]{2,1,0:T(8,128)(2,1)} %param.6) | copy-start | bytes 4718596
  267.3 81.8 %all-to-all-start = ((bf16[64,2,8,1536]{3,2,1,0:T(8,128)(2,1)}), bf16[64,2,8,1536]{3,2,1,0:T(8,128)(2,1)S(1)}, u32[]{:S(2)}, u32[]{:S(2)}) async-start(bf16[64,2,8,1536]{3,2,1,0:T(8,128)(2,1)} %select_select_fusion), calls=%async_computation | async-start | bytes 6291456 | tf_op jit(solution)/shard_map/all_to_all | solution.py:76
Sparse Core Ops, SparseCore 0:
  16.5 153.3 reduce-scatter.3
  172.6 82.6 all-gather.2
  257.7 41.6 all-reduce.3
  302.3 85.5 all-gather.4
where the time goes:
time: 409 us; the launch traced here: 408 us
  waiting for transfers between devices  343 us (84%)
  matrix products  18.6 us (5%)
  other arithmetic  16.2 us (4%)
  between operations  14 us (3%)
  local copies, waits for them, and re-layouts  10.4 us (3%)
  starting transfers between devices  6.46 us (2%)
    unnamed x5, waiting for transfers between devices  154 us
    all_gather x1, waiting for transfers between devices, body(): lax.all_gather(proj_weight, 'fsdp', axis=0, tiled=True)  83 us
    all_to_all x1, waiting for transfers between devices, body(): lax.all_to_all(send_rows.reshape(group_size, capacity, SEG, D), 'fsdp', s...  48.2 us
    all_gather x1, waiting for transfers between devices, stem_taps(): lax.all_gather(stem_weight, 'fsdp', axis=1, tiled=True)  36.3 us
    psum x1, waiting for transfers between devices, body(): shard_sum = lax.psum(shard_sum, 'site')  21.2 us
    dot_general x1, matrix products, stem_taps(): jnp.einsum('rd,kcd->krc', frames, lax.all_gather(stem_weight, 'fsdp', axi...  8.38 us
  transfers between devices with their start and end apart: 5, of which 5 were waited for; matrix products, arithmetic and copies ran while one was open for 5% of the time, Pallas kernels for 0%

commit v1 on v0

--- a/solution.py
+++ b/solution.py
@@ -34,7 +34,9 @@
     normed_bf = normed.astype(jnp.bfloat16)
     proj_back = lax.dot_general(
         cotangent,
-        lax.all_gather(proj_weight, "fsdp", axis=0, tiled=True),
+        jnp.concatenate(
+            lax.all_to_all(jnp.stack([proj_weight] * lax.axis_size("fsdp")), "fsdp", 0, 0), axis=0
+        ),
         (((1,), (1,)), ((), ())),
         preferred_element_type=jnp.float32,
     )

time: 409 us -> 355 us (0.87)
  waiting for transfers between devices: 343 us -> 266 us
  starting transfers between devices: 6.46 us -> 26 us
    all_gather x1 -> x0, waiting for transfers between devices: 83 us -> none  [body(): lax.all_gather(proj_weight, 'fsdp', axis=0, tiled=True)]
    all_to_all x0 -> x1, starting transfers between devices: none -> 13.5 us  [body(): lax.all_to_all(jnp.stack([proj_weight] * lax.axis_size('fsdp')), 'fsdp',...]
    unnamed x5 -> x4, waiting for transfers between devices: 154 us -> 163 us
    all_to_all x1, starting transfers between devices: 6.3 us -> 12.4 us  [body(): lax.all_to_all(send_rows.reshape(group_size, capacity, SEG, D), 'fsdp', s...]
  transfers between devices with their start and end apart: 5 -> 5, of which waited for: 5 -> 4; matrix products, arithmetic and copies ran while one was open for 5% -> 7% of each run, Pallas kernels for 0% -> 0%
where the time goes in v1:
time: 355 us
  waiting for transfers between devices  266 us (75%)
  starting transfers between devices  26 us (7%)
  matrix products  18.6 us (5%)
  other arithmetic  16.2 us (5%)
  between operations  14 us (4%)
  local copies, waits for them, and re-layouts  13.7 us (4%)
    unnamed x4, waiting for transfers between devices  163 us
    all_to_all x1, waiting for transfers between devices, body(): lax.all_to_all(send_rows.reshape(group_size, capacity, SEG, D), 'fsdp', s...  50.7 us
    all_gather x1, waiting for transfers between devices, stem_taps(): lax.all_gather(stem_weight, 'fsdp', axis=1, tiled=True)  33.8 us
    psum x1, waiting for transfers between devices, body(): shard_sum = lax.psum(shard_sum, 'site')  18.3 us
    all_to_all x1, starting transfers between devices, body(): lax.all_to_all(jnp.stack([proj_weight] * lax.axis_size('fsdp')), 'fsdp',...  13.5 us
    all_to_all x1, starting transfers between devices, body(): lax.all_to_all(send_rows.reshape(group_size, capacity, SEG, D), 'fsdp', s...  12.4 us
    dot_general x1, matrix products, stem_taps(): jnp.einsum('rd,kcd->krc', frames, lax.all_gather(stem_weight, 'fsdp', axi...  8.38 us
  transfers between devices with their start and end apart: 5, of which 4 were waited for; matrix products, arithmetic and copies ran while one was open for 7% of the time, Pallas kernels for 0%

profile of v1, /device:TPU:1, one launch (start us, length us, event | category | flops | bytes accessed | tf_op | source)
XLA Modules:
  0.0 354.7 jit_solution(15372905510068725123)
XLA Ops:
  7.2 1.8 convert_reduce_fusion
  9.1 2.0 fusion.10
  11.1 5.3 %fusion.25 = f32[1536,1536]{1,0:T(8,128)} fusion(bf16[1,512,1536]{2,1,0:T(8,128)(2,1)S(1)} %copy-done, bf16[1,512,1536]{2,1,0:T(8,128)(2,1)S(1)} %copy-done.1, f32[512]{0:T(512)S(1)} %add_rsqrt_fusion, f32[512]{0:T(512)S(1)} %broadcast_multiply_fusion.3), kind=kOutput, calls=%fused_computation.33 | convolution fusion | flops 2419064832 | bytes 12587008 | tf_op jit(solution)/shard_map/dot_general | solution.py:98
  16.4 0.9 copy-done.3
  17.3 2.4 stack.8
  19.7 13.5 %all-to-all-start = ((bf16[64,24,1536]{2,1,0:T(8,128)(2,1)}), bf16[64,24,1536]{2,1,0:T(8,128)(2,1)}, u32[]{:S(2)}, u32[]{:S(2)}) async-start(bf16[64,24,1536]{2,1,0:T(8,128)(2,1)} %stack.8), calls=%async_computation | async-start | bytes 9437184 | tf_op jit(solution)/shard_map/all_to_all | solution.py:38
  33.2 162.6 %reduce-scatter.4.cloned.1.call-done = f32[24,1536]{1,0:T(8,128)} async-done(((f32[1536,1536]{1,0:T(8,128)}), f32[24,1536]{1,0:T(8,128)}) %reduce-scatter.4.cloned.1.call-update) | async-done | bytes 147472
  195.9 0.7 all-gather.2.cloned.1.call-update
  198.5 4.9 %fusion.55 = (f32[512]{0:T(512)S(1)}, f32[512]{0:T(512)S(1)}, f32[512,1536]{1,0:T(8,128)S(1)}) fusion(f32[512]{0:T(512)S(1)} %add_rsqrt_fusion, f32[512]{0:T(512)S(1)} %broadcast_multiply_fusion.3, bf16[1,512,1536]{2,1,0:T(8,128)(2,1)S(1)} %copy-done, bf16[1536,1536]{1,0:T(8,128)(2,1)} %bitcast.4, bf16[1,512,1536]{2,1,0:T(8,128)(2,1)S(1)} %copy-done.1), kind=kOutput, calls=%fused_computation.107 | convolution fusion | flops 2420636672 | bytes 11018240 | tf_op jit(solution)/shard_map/dot_general | solution.py:35
  203.4 1.2 fusion.27
  204.6 2.5 gather_fusion
  207.1 3.3 select_select_fusion
  210.4 12.4 %all-to-all-start.1 = ((bf16[64,2,8,1536]{3,2,1,0:T(8,128)(2,1)}), bf16[64,2,8,1536]{3,2,1,0:T(8,128)(2,1)S(1)}, u32[]{:S(2)}, u32[]{:S(2)}) async-start(bf16[64,2,8,1536]{3,2,1,0:T(8,128)(2,1)} %select_select_fusion), calls=%async_computation.1 | async-start | bytes 6291456 | tf_op jit(solution)/shard_map/all_to_all | solution.py:78
  223.5 0.7 and_select_fusion.4
  224.3 1.3 compare_and_fusion.1
  226.0 1.3 fusion.52
  227.4 18.3 %all-reduce.4.cloned.1.call-done = f32[24,1536]{1,0:T(8,128)} async-done(((f32[24,1536]{1,0:T(8,128)}), f32[24,1536]{1,0:T(8,128)}) %all-reduce.4.cloned.1.call-update) | async-done | bytes 147472 | tf_op jit(solution)/shard_map/psum | solution.py:105
  245.7 1.6 broadcast_multiply_fusion
  247.3 50.7 %all-to-all-done.1 = bf16[64,2,8,1536]{3,2,1,0:T(8,128)(2,1)S(1)} async-done(((bf16[64,2,8,1536]{3,2,1,0:T(8,128)(2,1)}), bf16[64,2,8,1536]{3,2,1,0:T(8,128)(2,1)S(1)}, u32[]{:S(2)}, u32[]{:S(2)}) %all-to-all-start.1) | async-done | bytes 3145760 | tf_op jit(solution)/shard_map/all_to_all | solution.py:78
  298.0 2.4 gather_fusion.1
  300.4 33.8 %all-gather.2.cloned.1.call-done = bf16[3,512,1536]{2,1,0:T(8,128)(2,1)} async-done(((bf16[3,8,1536]{2,1,0:T(8,128)(2,1)}), bf16[3,512,1536]{2,1,0:T(8,128)(2,1)}) %all-gather.2.cloned.1.call-update) | async-done | bytes 4718608 | tf_op jit(solution)/shard_map/all_gather | solution.py:18
  334.3 8.4 %fusion.19 = f32[3,1024,512]{2,1,0:T(8,128)S(1)} fusion(bf16[3,512,1536]{2,1,0:T(8,128)(2,1)} %all-gather.2.cloned.1.call-done, bf16[128,8,1536]{2,1,0:T(8,128)(2,1)} %gather_fusion.1, pred[1024]{0:T(1024)(128)(4,1)S(1)} %broadcast_in_dim.96, pred[1024]{0:T(1024)(128)(4,1)S(1)} %broadcast_in_dim.93), kind=kOutput, calls=%fused_computation.25 | convolution fusion | flops 4834983936 | bytes 14157824 | tf_op jit(solution)/shard_map/rd,kcd->krc/dot_general | solution.py:15
  343.8 2.2 copy.13
  346.0 2.2 convert_element_type.46
  (43 shorter events, 4.3 us)
Async XLA Ops:
  7.2 3.9 %copy-start = (bf16[1,512,1536]{2,1,0:T(8,128)(2,1)S(1)}, bf16[1,512,1536]{2,1,0:T(8,128)(2,1)}, u32[]{:S(2)}) copy-start(bf16[1,512,1536]{2,1,0:T(8,128)(2,1)} %param.5) | copy-start | bytes 4718596
  7.2 3.9 %copy-start.1 = (bf16[1,512,1536]{2,1,0:T(8,128)(2,1)S(1)}, bf16[1,512,1536]{2,1,0:T(8,128)(2,1)}, u32[]{:S(2)}) copy-start(bf16[1,512,1536]{2,1,0:T(8,128)(2,1)} %param.6) | copy-start | bytes 4718596
  7.2 188.6 %reduce-scatter.4.cloned.1.call-start = ((), (), s32[]{:S(2)}) async-start(), calls=%async_computation.5 | async-start | bytes 9584640
  16.4 0.9 copy-start.3
  19.7 176.9 %copy-start.4 = (s32[1,64]{1,0:T(1,128)S(1)}, s32[1,64]{1,0:T(1,128)}, u32[]{:S(2)}) copy-start(s32[1,64]{1,0:T(1,128)} %param.9) | copy-start | bytes 772
  19.7 178.8 %all-to-all-start = ((bf16[64,24,1536]{2,1,0:T(8,128)(2,1)}), bf16[64,24,1536]{2,1,0:T(8,128)(2,1)}, u32[]{:S(2)}, u32[]{:S(2)}) async-start(bf16[64,24,1536]{2,1,0:T(8,128)(2,1)} %stack.8), calls=%async_computation | async-start | bytes 9437184 | tf_op jit(solution)/shard_map/all_to_all | solution.py:38
  33.2 212.6 %all-reduce.4.cloned.1.call-start = ((), (), s32[]{:S(2)}) async-start(), calls=%async_computation.4 | async-start | bytes 294912 | tf_op jit(solution)/shard_map/psum | solution.py:105
  195.9 138.4 %all-gather.2.cloned.1.call-start = ((), (), s32[]{:S(2)}) async-start(), calls=%async_computation.3 | async-start | bytes 4792320 | tf_op jit(solution)/shard_map/all_gather | solution.py:18
  198.5 4.9 %copy-start.2 = (bf16[1,512,1536]{2,1,0:T(8,128)(2,1)S(1)}, bf16[1,512,1536]{2,1,0:T(8,128)(2,1)}, u32[]{:S(2)}) copy-start(bf16[1,512,1536]{2,1,0:T(8,128)(2,1)} %param.6) | copy-start | bytes 4718596
  210.4 87.6 %all-to-all-start.1 = ((bf16[64,2,8,1536]{3,2,1,0:T(8,128)(2,1)}), bf16[64,2,8,1536]{3,2,1,0:T(8,128)(2,1)S(1)}, u32[]{:S(2)}, u32[]{:S(2)}) async-start(bf16[64,2,8,1536]{3,2,1,0:T(8,128)(2,1)} %select_select_fusion), calls=%async_computation.1 | async-start | bytes 6291456 | tf_op jit(solution)/shard_map/all_to_all | solution.py:78
Sparse Core Ops, SparseCore 0:
  16.5 179.2 reduce-scatter.3
  198.2 47.5 all-reduce.3
  248.8 85.4 all-gather.1
